TPU v7x, 32 devices: a whole 2x2x4 slice. The times are simulated.
32 devices in a mesh: grp: 4 (over x, core), mem: 8 (over z, y).
Axes of the slice: x: 2, y: 2, z: 4, core: 2. Of those that a mesh axis runs over, the one named last changes fastest.
Arguments:
- perturb: float32 [32, 1024, 1024], P(('grp', 'mem')), may hold values from -0.1875 to 0.1875
- touched_vertex_index: int32 [32, 4, 64], P(('grp', 'mem')), may hold values from 0 to 1023
- proposed_spin_values: int32 [32, 4, 64], P(('grp', 'mem')), may hold values from 0 to 1
- accept: int32 [32, 4, 64], P(('grp', 'mem')), may hold values 0 or 1
- vertex_site_index: int32 [32, 1024], P(('grp', 'mem')), may hold values from 0 to 63
- vertex_time_index: int32 [32, 1024], P(('grp', 'mem')), may hold values from 0 to 4095
- left_proj: float32 [64, 1024], replicated, may hold values from -0.06 to 0.06
- right_proj: float32 [64, 1024], replicated, may hold values from -0.06 to 0.06
- weights: float32 [32], P(('grp', 'mem')), may hold values from 0.3 to 3
- routing: int32 [32, 1], P(('grp', 'mem')), may hold values from 0 to 7; in each aligned block of 8 rows (0 to 7, 8 to 15, ...) at most 2 rows name the same one
- vertex_function_total: float32 [16, 4096, 4096], P('grp', 'mem'), may hold values from -6 to 6
Outputs:
- four_point_out: float32 [16, 4096, 4096], P('grp', 'mem')
Inputs may be any that keep to these rules, and one draw needn't show every extreme that they name: `routing`: among the 8 walkers of one group no member index is named by more than 2 walkers, and in some group one index is named by exactly 2.
All inputs are finite; a program needn't handle non-finite values. No bound on the sum of `accept` on one device may be relied on, other than what follows from the above.
Results may differ from a plain program's by a relative error of at most 0.0003.
Values sent between devices are 32-bit elements; how exact they have to be, the bound alone decides.
A program may use at most 128 MiB of HBM per device.

v0:
```python
import jax
import jax.numpy as jnp
from jax import lax
from jax.sharding import PartitionSpec as P

K = 1024
SITES = 64
LEG = 64
Q = 16
TIMES = 4096
UPDATES = 4
EXACT_ARITHMETIC = lax.Precision.HIGHEST


def legendre(time_ids):
    abscissa = (2.0 * time_ids.astype(jnp.float32) + 1.0) / TIMES - 1.0
    polys = [jnp.ones_like(abscissa), abscissa]
    for degree in range(1, LEG - 1):
        polys.append(
            ((2 * degree + 1) * abscissa * polys[degree] - degree * polys[degree - 1])
            / (degree + 1)
        )
    norms = jnp.sqrt(2.0 * jnp.arange(LEG, dtype=jnp.float32) + 1.0)
    return jnp.stack(polys[:LEG], axis=1) * norms[None, :]


def make_onehot(site_ids):
    return (site_ids[:, None] == jnp.arange(SITES, dtype=jnp.int32)[None, :]).astype(jnp.float32)


def project(onehot, polys, table):
    spread = jnp.dot(onehot, table, precision=EXACT_ARITHMETIC, preferred_element_type=jnp.float32)
    return jnp.sum(spread.reshape(-1, LEG, Q) * polys[:, :, None], axis=1)


def transform(onehot, polys, values):
    weighted = (polys[:, :, None] * values[:, None, :]).reshape(-1, LEG * Q)
    summed = jnp.dot(
        onehot.T, weighted, precision=EXACT_ARITHMETIC, preferred_element_type=jnp.float32
    )
    return summed.reshape(SITES, LEG, Q).transpose(2, 0, 1).reshape(Q, SITES * LEG)


def update_walker(perturb, touched_vertex_index, proposed_spin_values, accept):
    matrix = jnp.eye(K, dtype=jnp.float32) + perturb
    gammas = accept.astype(jnp.float32) * jnp.where(proposed_spin_values == 1, 0.6, -0.4).astype(
        jnp.float32
    )
    positions = jnp.arange(K, dtype=jnp.int32)

    def apply_update(update, matrix):
        chosen = touched_vertex_index[update]
        unit_cols = (positions[:, None] == chosen[None, :]).astype(jnp.float32)
        columns = (jnp.take(matrix, chosen, axis=1) - unit_cols) * gammas[update][None, :]
        row_block = jnp.take(matrix, chosen, axis=0)
        return matrix - jnp.dot(
            columns, row_block, precision=EXACT_ARITHMETIC, preferred_element_type=jnp.float32
        )

    return lax.fori_loop(0, UPDATES, apply_update, matrix)


def reduce_measured_rows(rescaled_rows, right_observed, vertex_function_total):
    left_q, right_q = (
        lax.all_to_all(rescaled_rows, "grp", split_axis=1, concat_axis=0, tiled=True),
        lax.all_to_all(right_observed, "grp", split_axis=1, concat_axis=0, tiled=True),
    )
    left_rows = lax.all_to_all(left_q, "mem", split_axis=2, concat_axis=0, tiled=True)
    return vertex_function_total + jnp.einsum(
        "mqr,mqc->qrc",
        left_rows,
        lax.all_gather(right_q, "mem", axis=0, tiled=True),
        precision=EXACT_ARITHMETIC,
    )


def per_device(
    perturb,
    touched_vertex_index,
    proposed_spin_values,
    accept,
    vertex_site_index,
    vertex_time_index,
    left_proj,
    right_proj,
    weights,
    routing,
    vertex_function_total,
):
    matrix = update_walker(perturb[0], touched_vertex_index[0], proposed_spin_values[0], accept[0])
    polys = legendre(vertex_time_index[0])
    onehot = make_onehot(vertex_site_index[0])
    left_vec = project(onehot, polys, left_proj)
    right_vec = project(onehot, polys, right_proj)
    left_image = jnp.dot(
        matrix, left_vec, precision=EXACT_ARITHMETIC, preferred_element_type=jnp.float32
    )
    right_image = jnp.dot(
        matrix.T, right_vec, precision=EXACT_ARITHMETIC, preferred_element_type=jnp.float32
    )
    member_mask = (jnp.arange(lax.axis_size("mem"), dtype=jnp.int32) == routing[0, 0]).astype(
        jnp.float32
    )
    totals = lax.psum(member_mask * weights[0], "mem")
    own_total = jnp.sum(totals * member_mask)
    gamma_factor_list = weights / own_total
    left_observed = transform(onehot, polys, left_image)[None]
    right_observed = transform(onehot, polys, right_image)[None]
    rescaled_rows = left_observed * gamma_factor_list[:, None, None]
    return reduce_measured_rows(rescaled_rows, right_observed, vertex_function_total)


def solution(mesh):
    in_specs = (
        P(("grp", "mem"), None, None),
        P(("grp", "mem"), None, None),
        P(("grp", "mem"), None, None),
        P(("grp", "mem"), None, None),
        P(("grp", "mem"), None),
        P(("grp", "mem"), None),
        P(),
        P(),
        P(("grp", "mem")),
        P(("grp", "mem"), None),
        P("grp", "mem", None),
    )
    out_specs = P("grp", "mem", None)
    return jax.shard_map(
        per_device, mesh=mesh, in_specs=in_specs, out_specs=out_specs, check_vma=False
    )
```

profile of v0, /device:TPU:0, one launch (start us, length us, event | category | flops | bytes accessed | tf_op | source)
XLA Modules:
  0.0 259.0 jit_solution(9554184018250131046)
XLA Ops:
  7.9 4.9 %bitcast_add_fusion = f32[1024,1024]{1,0:T(8,128)} fusion(f32[1,1024,1024]{2,1,0:T(8,128)} %param.13), kind=kLoop, calls=%fused_computation.24 | loop fusion | flops 3145728 | bytes 8388608 | tf_op jit(solution)/shard_map/add | solution.py:45
  12.8 73.3 %while.14 = (s32[]{:T(128)}, f32[1024,1024]{1,0:T(8,128)}, s32[4,64]{1,0:T(4,128)S(1)}, f32[4,64]{1,0:T(4,128)S(1)}, s32[]{:T(128)}) while((s32[]{:T(128)}, f32[1024,1024]{1,0:T(8,128)}, s32[4,64]{1,0:T(4,128)S(1)}, f32[4,64]{1,0:T(4,128)S(1)}, s32[]{:T(128)}) %tuple.131), condition=%wide.region_1.2_spmd.clone, body=%wide.region_0.1_spmd.clone.sunk | while | flops 806749760 | bytes 18357200 | solution.py:60
  15.9 5.4 %copy.43 = f32[1024,1024]{0,1:T(8,128)} copy(f32[1024,1024]{1,0:T(8,128)} %get-tuple-element.275) | data formatting | bytes 8388608 | tf_op jit(solution)/shard_map/while
  24.2 6.8 %convolution_subtract_fusion.2 = f32[1024,1024]{1,0:T(8,128)} fusion(f32[1024,1024]{1,0:T(8,128)} %get-tuple-element.275, f32[64,1024]{1,0:T(8,128)S(1)} %gather_fusion, f32[64,1024]{1,0:T(8,128)S(1)} %gather_fusion.1, f32[64]{0:T(128)S(1)} %dynamic-slice_bitcast_fusion.2, s32[64]{0:T(128)S(1)} %get-tuple-element.267, ...), kind=kOutput, calls=%fused_computation.3.clone.1 | convolution fusion | flops 806748160 | bytes 8913472 | tf_op jit(solution)/shard_map/while/body/eval_jaxpr/dot_general | solution.py:56
  34.1 5.4 %copy.43 = f32[1024,1024]{0,1:T(8,128)} copy(f32[1024,1024]{1,0:T(8,128)} %get-tuple-element.275) | data formatting | bytes 8388608 | tf_op jit(solution)/shard_map/while
  42.4 6.8 %convolution_subtract_fusion.2 = f32[1024,1024]{1,0:T(8,128)} fusion(f32[1024,1024]{1,0:T(8,128)} %get-tuple-element.275, f32[64,1024]{1,0:T(8,128)S(1)} %gather_fusion, f32[64,1024]{1,0:T(8,128)S(1)} %gather_fusion.1, f32[64]{0:T(128)S(1)} %dynamic-slice_bitcast_fusion.2, s32[64]{0:T(128)S(1)} %get-tuple-element.267, ...), kind=kOutput, calls=%fused_computation.3.clone.1 | convolution fusion | flops 806748160 | bytes 8913472 | tf_op jit(solution)/shard_map/while/body/eval_jaxpr/dot_general | solution.py:56
  52.3 5.4 %copy.43 = f32[1024,1024]{0,1:T(8,128)} copy(f32[1024,1024]{1,0:T(8,128)} %get-tuple-element.275) | data formatting | bytes 8388608 | tf_op jit(solution)/shard_map/while
  60.6 6.8 %convolution_subtract_fusion.2 = f32[1024,1024]{1,0:T(8,128)} fusion(f32[1024,1024]{1,0:T(8,128)} %get-tuple-element.275, f32[64,1024]{1,0:T(8,128)S(1)} %gather_fusion, f32[64,1024]{1,0:T(8,128)S(1)} %gather_fusion.1, f32[64]{0:T(128)S(1)} %dynamic-slice_bitcast_fusion.2, s32[64]{0:T(128)S(1)} %get-tuple-element.267, ...), kind=kOutput, calls=%fused_computation.3.clone.1 | convolution fusion | flops 806748160 | bytes 8913472 | tf_op jit(solution)/shard_map/while/body/eval_jaxpr/dot_general | solution.py:56
  70.5 5.4 %copy.43 = f32[1024,1024]{0,1:T(8,128)} copy(f32[1024,1024]{1,0:T(8,128)} %get-tuple-element.275) | data formatting | bytes 8388608 | tf_op jit(solution)/shard_map/while
  78.9 6.8 %convolution_subtract_fusion.2 = f32[1024,1024]{1,0:T(8,128)} fusion(f32[1024,1024]{1,0:T(8,128)} %get-tuple-element.275, f32[64,1024]{1,0:T(8,128)S(1)} %gather_fusion, f32[64,1024]{1,0:T(8,128)S(1)} %gather_fusion.1, f32[64]{0:T(128)S(1)} %dynamic-slice_bitcast_fusion.2, s32[64]{0:T(128)S(1)} %get-tuple-element.267, ...), kind=kOutput, calls=%fused_computation.3.clone.1 | convolution fusion | flops 806748160 | bytes 8913472 | tf_op jit(solution)/shard_map/while/body/eval_jaxpr/dot_general | solution.py:56
  86.2 3.8 %fusion.28 = f32[1024,1024]{0,1:T(8,128)} fusion(f32[64,1024]{1,0:T(8,128)S(1)} %copy-done, s32[1024]{0:T(1024)S(1)} %bitcast.184), kind=kOutput, calls=%fused_computation.39 | convolution fusion | flops 805371904 | bytes 4460544 | tf_op jit(solution)/shard_map/dot_general | solution.py:32
  90.0 3.8 %fusion.30 = f32[1024,1024]{0,1:T(8,128)} fusion(f32[64,1024]{1,0:T(8,128)S(1)} %copy-done.3, s32[1024]{0:T(1024)S(1)} %bitcast.185), kind=kOutput, calls=%fused_computation.41 | convolution fusion | flops 805371904 | bytes 4460544 | tf_op jit(solution)/shard_map/dot_general | solution.py:32
  94.8 4.7 %multiply_reduce_fusion = (f32[1024,16]{0,1:T(8,128)S(1)}, f32[1024,16]{0,1:T(8,128)S(1)}) fusion(f32[1024,64,16]{0,2,1:T(8,128)} %bitcast.178, f32[1024,64]{0,1:T(8,128)S(1)} %broadcast_multiply_fusion, f32[1024,64,16]{0,2,1:T(8,128)} %bitcast.179), kind=kLoop, calls=%fused_computation.30 | loop fusion | flops 4161536 | bytes 8781824 | tf_op jit(solution)/shard_map/reduce_sum | solution.py:33
  108.1 5.6 %fusion.19 = f32[16,64,64]{2,1,0:T(8,128)S(1)} fusion(f32[64,16,1024]{2,1,0:T(8,128)S(1)} %get-tuple-element.173, s32[1024]{0:T(1024)S(1)} %bitcast.186), kind=kOutput, calls=%fused_computation.35 | convolution fusion | flops 805371904 | bytes 4460544 | tf_op jit(solution)/shard_map/dot_general | solution.py:38
  114.0 10.0 %all_to_all.42 = f32[1,16,4096]{2,0,1:T(1,128)S(1)} all-to-all(f32[1,16,4096]{2,0,1:T(1,128)S(1)} %broadcast_in_dim_reshape.5), channel_id=1, replica_groups=mesh['grp'=4,'mem'=8] {'grp'}, dimensions={1} | all-to-all | bytes 524288 | tf_op jit(solution)/shard_map/all_to_all | solution.py:66
  126.8 21.8 %psum.7 = f32[8]{0:T(128)S(1)} all-reduce(f32[8]{0:T(128)S(1)} %compare_select_fusion.3), channel_id=1, replica_groups=mesh['grp'=4,'mem'=8] {'mem'}, use_global_device_ids=true, to_apply=%region_3.4 | all-reduce | flops 8 | bytes 64 | tf_op jit(solution)/shard_map/psum | solution.py:104
  150.0 7.4 %fusion.25 = f32[16,64,64]{2,1,0:T(8,128)S(1)} fusion(f32[64,16,1024]{2,1,0:T(8,128)} %get-tuple-element.174, f32[]{:T(128)} %bitcast.34, s32[1024]{0:T(1024)S(1)} %bitcast.187), kind=kOutput, calls=%fused_computation.37 | convolution fusion | flops 805437440 | bytes 4460548 | tf_op jit(solution)/shard_map/dot_general | solution.py:38
  157.7 8.6 %all_to_all.43 = f32[1,16,4096]{2,0,1:T(1,128)S(1)} all-to-all(f32[1,16,4096]{2,0,1:T(1,128)S(1)} %mul.18371), channel_id=1, replica_groups=mesh['grp'=4,'mem'=8] {'grp'}, dimensions={1} | all-to-all | bytes 524288 | tf_op jit(solution)/shard_map/all_to_all | solution.py:65
  167.0 5.8 %copy.21 = f32[4,4,4096]{1,0,2:T(4,128)} copy(f32[4,4,4096]{2,1,0:T(4,128)S(1)} %all_to_all.32) | data formatting | bytes 524288 | tf_op jit(solution)/shard_map/all_to_all | solution.py:65
  172.8 11.3 %reshape.1435 = f32[8,1,8192]{2,1,0:T(1,128)S(1)} reshape(f32[4096,4,4]{2,1,0:T(4,128)} %bitcast.176) | data formatting | bytes 524288
  184.1 11.6 %all_to_all.44 = f32[8,1,8192]{2,1,0:T(1,128)S(1)} all-to-all(f32[8,1,8192]{2,1,0:T(1,128)S(1)} %reshape.1435), channel_id=1, replica_groups=mesh['grp'=4,'mem'=8] {'mem'}, dimensions={0} | all-to-all | bytes 524288 | tf_op jit(solution)/shard_map/all_to_all | solution.py:68
  197.6 14.2 %reshape.1436 = f32[4096,4,4]{2,1,0:T(4,128)} reshape(f32[8,8192]{1,0:T(8,128)S(1)} %reduce.2) | data formatting | bytes 524288
  211.8 5.2 %copy.27 = f32[4,4,8,512]{3,2,1,0:T(8,128)S(1)} copy(f32[4,4,8,512]{1,0,3,2:T(4,128)} %bitcast.177) | data formatting | bytes 524288 | tf_op jit(solution)/shard_map/all_to_all | solution.py:68
  217.3 34.6 %convolution_add_fusion = f32[4,512,4096]{2,1,0:T(8,128)} fusion(f32[4,512,4096]{2,1,0:T(8,128)} %param.23, f32[32,4,512]{2,0,1:T(8,128)S(1)} %all_to_all.36, f32[32,4,4096]{2,1,0:T(4,128)} %all-gather.2.cloned.1.call-done), kind=kOutput, calls=%fused_computation.23 | convolution fusion | flops 3229614080 | bytes 69468160 | tf_op jit(solution)/shard_map/mqr,mqc->qrc/dot_general | solution.py:69
  (86 shorter events, 40.2 us)
Async XLA Ops:
  6.5 79.6 %copy-start = (f32[64,1024]{1,0:T(8,128)S(1)}, f32[64,1024]{1,0:T(8,128)}, u32[]{:S(2)}) copy-start(f32[64,1024]{1,0:T(8,128)} %param.20) | copy-start | bytes 786436
  6.5 210.8 %all-gather.2.cloned.1.call-start = ((), (), s32[]{:S(2)}) async-start(), calls=%async_computation.3 | async-start | bytes 2359296 | tf_op jit(solution)/shard_map/all_gather | solution.py:72
  7.8 4.9 %copy-start.6 = (s32[1,4,64]{2,1,0:T(4,128)S(1)}, s32[1,4,64]{2,1,0:T(4,128)}, u32[]{:S(2)}) copy-start(s32[1,4,64]{2,1,0:T(4,128)} %param.16) | copy-start | bytes 3076
  7.8 4.9 %copy-start.7 = (s32[1,4,64]{2,1,0:T(4,128)S(1)}, s32[1,4,64]{2,1,0:T(4,128)}, u32[]{:S(2)}) copy-start(s32[1,4,64]{2,1,0:T(4,128)} %param.15) | copy-start | bytes 3076
  7.9 4.9 %copy-start.5 = (s32[1,4,64]{2,1,0:T(4,128)S(1)}, s32[1,4,64]{2,1,0:T(4,128)}, u32[]{:S(2)}) copy-start(s32[1,4,64]{2,1,0:T(4,128)} %param.14) | copy-start | bytes 3076
  12.8 73.4 %copy-start.4 = (s32[1,1024]{1,0:T(1,128)S(1)}, s32[1,1024]{1,0:T(1,128)}, u32[]{:S(2)}) copy-start(s32[1,1024]{1,0:T(1,128)} %param.17) | copy-start | bytes 12292
  86.1 3.8 %copy-start.3 = (f32[64,1024]{1,0:T(8,128)S(1)}, f32[64,1024]{1,0:T(8,128)}, u32[]{:S(2)}) copy-start(f32[64,1024]{1,0:T(8,128)} %param.19) | copy-start | bytes 786436
  94.8 4.7 %copy-start.2 = (f32[1024,1024]{1,0:T(8,128)S(1)}, f32[1024,1024]{1,0:T(8,128)}, u32[]{:S(2)}) copy-start(f32[1024,1024]{1,0:T(8,128)} %get-tuple-element.99) | copy-start | bytes 12582916
  217.3 34.6 %copy-start.1 = (f32[64,1024]{1,0:T(8,128)S(1)}, f32[64,1024]{1,0:T(8,128)}, u32[]{:S(2)}) copy-start(f32[64,1024]{1,0:T(8,128)} %param.20) | copy-start | bytes 786436
Sparse Core Ops, SparseCore 0:
  125.6 49.6 all-gather.1
where the time goes:
time: 263 us; the launch traced here: 259 us
  matrix products  88.3 us (34%)
  local copies, waits for them, and re-layouts  84.9 us (32%)
  blocking collectives  52.1 us (20%)
  other arithmetic  17.1 us (7%)
  between operations  16 us (6%)
    dot_general x1, matrix products, reduce_measured_rows(): jnp.einsum('mqr,mqc->qrc', left_rows, lax.all_gather(right_q, 'mem', axis...  34.6 us
    dot_general x4, matrix products, apply_update(): jnp.dot(columns, row_block, precision=EXACT_ARITHMETIC, preferred_element...  27.2 us
    unnamed x18, local copies, waits for them, and re-layouts  25.6 us
    psum x1, blocking collectives, per_device(): totals = lax.psum(member_mask * weights[0], 'mem')  21.8 us
    while x4, local copies, waits for them, and re-layouts  21.6 us
    dot_general x2, matrix products, transform(): jnp.dot(onehot.T, weighted, precision=EXACT_ARITHMETIC, preferred_element...  13 us
    gather x4, local copies, waits for them, and re-layouts, apply_update(): row_block = jnp.take(matrix, chosen, axis=0)  11.9 us
    gather x4, local copies, waits for them, and re-layouts, apply_update(): jnp.take(matrix, chosen, axis=1) - unit_cols  11.9 us
  transfers between devices with their start and end apart: 1, of which 0 were waited for; matrix products, arithmetic and copies ran while one was open for 18% of the time, Pallas kernels for 0%

commit v1 on v0

--- a/solution.py
+++ b/solution.py
@@ -65,7 +65,10 @@
         lax.all_to_all(rescaled_rows, "grp", split_axis=1, concat_axis=0, tiled=True),
         lax.all_to_all(right_observed, "grp", split_axis=1, concat_axis=0, tiled=True),
     )
-    left_rows = lax.all_to_all(left_q, "mem", split_axis=2, concat_axis=0, tiled=True)
+    left_rows = jnp.concatenate(
+        lax.all_to_all(jnp.stack(jnp.split(left_q, lax.axis_size("mem"), axis=2)), "mem", 0, 0),
+        axis=0,
+    )
     return vertex_function_total + jnp.einsum(
         "mqr,mqc->qrc",
         left_rows,

time: 263 us -> 222 us (0.84); the launches traced: 259 us -> 221 us
  local copies, waits for them, and re-layouts: 84.9 us -> 47.6 us
    unnamed x18 -> x23, local copies, waits for them, and re-layouts: 25.6 us -> 0.2 us
    all_to_all x4 -> x1, local copies, waits for them, and re-layouts: 6.01 us -> 0.02 us  [reduce_measured_rows(): lax.all_to_all(jnp.stack(jnp.split(left_q, lax.axis_size('mem'), axis=2))...]
    all_to_all x2 -> x1, local copies, waits for them, and re-layouts: 5.92 us -> 0.08 us  [reduce_measured_rows(): lax.all_to_all(rescaled_rows, 'grp', split_axis=1, concat_axis=0, tiled=T...]
  transfers between devices with their start and end apart: 1 -> 1, of which waited for: 0 -> 0; matrix products, arithmetic and copies ran while one was open for 18% -> 4% of each run, Pallas kernels for 0% -> 0%
where the time goes in v1:
time: 222 us; the launch traced here: 221 us
  matrix products  88.1 us (40%)
  blocking collectives  53.8 us (24%)
  local copies, waits for them, and re-layouts  47.6 us (21%)
  other arithmetic  15.9 us (7%)
  between operations  15.8 us (7%)
    dot_general x1, matrix products, reduce_measured_rows(): jnp.einsum('mqr,mqc->qrc', left_rows, lax.all_gather(right_q, 'mem', axis...  34.4 us
    dot_general x4, matrix products, apply_update(): jnp.dot(columns, row_block, precision=EXACT_ARITHMETIC, preferred_element...  27.1 us
    psum x1, blocking collectives, per_device(): totals = lax.psum(member_mask * weights[0], 'mem')  21.8 us
    while x4, local copies, waits for them, and re-layouts  21.4 us
    all_to_all x1, blocking collectives, reduce_measured_rows(): lax.all_to_all(jnp.stack(jnp.split(left_q, lax.axis_size('mem'), axis=2))...  13.6 us
    dot_general x2, matrix products, transform(): jnp.dot(onehot.T, weighted, precision=EXACT_ARITHMETIC, preferred_element...  13 us
    gather x4, local copies, waits for them, and re-layouts, apply_update(): row_block = jnp.take(matrix, chosen, axis=0)  11.9 us
    gather x4, local copies, waits for them, and re-layouts, apply_update(): jnp.take(matrix, chosen, axis=1) - unit_cols  11.9 us
  transfers between devices with their start and end apart: 1, of which 0 were waited for; matrix products, arithmetic and copies ran while one was open for 4% of the time, Pallas kernels for 0%

profile of v1, /device:TPU:0, one launch (start us, length us, event | category | flops | bytes accessed | tf_op | source)
XLA Modules:
  0.0 221.4 jit_solution(5353907965545448806)
XLA Ops:
  7.9 4.9 %bitcast_add_fusion = f32[1024,1024]{1,0:T(8,128)} fusion(f32[1,1024,1024]{2,1,0:T(8,128)} %param.13), kind=kLoop, calls=%fused_computation.24 | loop fusion | flops 3145728 | bytes 8388608 | tf_op jit(solution)/shard_map/add | solution.py:45
  12.8 72.7 %while.14 = (s32[]{:T(128)}, f32[1024,1024]{1,0:T(8,128)}, s32[4,64]{1,0:T(4,128)S(1)}, f32[4,64]{1,0:T(4,128)S(1)}, s32[]{:T(128)}) while((s32[]{:T(128)}, f32[1024,1024]{1,0:T(8,128)}, s32[4,64]{1,0:T(4,128)S(1)}, f32[4,64]{1,0:T(4,128)S(1)}, s32[]{:T(128)}) %tuple.138), condition=%wide.region_1.2_spmd.clone, body=%wide.region_0.1_spmd.clone.sunk | while | flops 806749760 | bytes 18357200 | solution.py:60
  12.9 3.0 %gather_fusion.1 = f32[64,1024]{1,0:T(8,128)S(1)} fusion(f32[1024,1024]{1,0:T(8,128)} %get-tuple-element.283, s32[1024]{0:T(1024)S(1)} %pad_clamp_fusion.2), kind=kCustom, calls=%fused_computation.1.clone.clone.1 | custom fusion | bytes 524544 | tf_op jit(solution)/shard_map/while/body/eval_jaxpr/jit(_take)/gather | solution.py:55
  15.9 5.4 %copy.95 = f32[1024,1024]{0,1:T(8,128)} copy(f32[1024,1024]{1,0:T(8,128)} %get-tuple-element.283) | data formatting | bytes 8388608 | tf_op jit(solution)/shard_map/while
  24.2 6.8 %convolution_subtract_fusion.2 = f32[1024,1024]{1,0:T(8,128)} fusion(f32[1024,1024]{1,0:T(8,128)} %get-tuple-element.283, f32[64,1024]{1,0:T(8,128)S(1)} %gather_fusion, f32[64,1024]{1,0:T(8,128)S(1)} %gather_fusion.1, f32[64]{0:T(128)S(1)} %dynamic-slice_bitcast_fusion.2, s32[64]{0:T(128)S(1)} %get-tuple-element.275, ...), kind=kOutput, calls=%fused_computation.3.clone.1 | convolution fusion | flops 806748160 | bytes 8913472 | tf_op jit(solution)/shard_map/while/body/eval_jaxpr/dot_general | solution.py:56
  31.0 3.0 %gather_fusion.1 = f32[64,1024]{1,0:T(8,128)S(1)} fusion(f32[1024,1024]{1,0:T(8,128)} %get-tuple-element.283, s32[1024]{0:T(1024)S(1)} %pad_clamp_fusion.2), kind=kCustom, calls=%fused_computation.1.clone.clone.1 | custom fusion | bytes 524544 | tf_op jit(solution)/shard_map/while/body/eval_jaxpr/jit(_take)/gather | solution.py:55
  34.0 5.4 %copy.95 = f32[1024,1024]{0,1:T(8,128)} copy(f32[1024,1024]{1,0:T(8,128)} %get-tuple-element.283) | data formatting | bytes 8388608 | tf_op jit(solution)/shard_map/while
  42.4 6.8 %convolution_subtract_fusion.2 = f32[1024,1024]{1,0:T(8,128)} fusion(f32[1024,1024]{1,0:T(8,128)} %get-tuple-element.283, f32[64,1024]{1,0:T(8,128)S(1)} %gather_fusion, f32[64,1024]{1,0:T(8,128)S(1)} %gather_fusion.1, f32[64]{0:T(128)S(1)} %dynamic-slice_bitcast_fusion.2, s32[64]{0:T(128)S(1)} %get-tuple-element.275, ...), kind=kOutput, calls=%fused_computation.3.clone.1 | convolution fusion | flops 806748160 | bytes 8913472 | tf_op jit(solution)/shard_map/while/body/eval_jaxpr/dot_general | solution.py:56
  49.2 3.0 %gather_fusion.1 = f32[64,1024]{1,0:T(8,128)S(1)} fusion(f32[1024,1024]{1,0:T(8,128)} %get-tuple-element.283, s32[1024]{0:T(1024)S(1)} %pad_clamp_fusion.2), kind=kCustom, calls=%fused_computation.1.clone.clone.1 | custom fusion | bytes 524544 | tf_op jit(solution)/shard_map/while/body/eval_jaxpr/jit(_take)/gather | solution.py:55
  52.2 5.4 %copy.95 = f32[1024,1024]{0,1:T(8,128)} copy(f32[1024,1024]{1,0:T(8,128)} %get-tuple-element.283) | data formatting | bytes 8388608 | tf_op jit(solution)/shard_map/while
  60.5 6.8 %convolution_subtract_fusion.2 = f32[1024,1024]{1,0:T(8,128)} fusion(f32[1024,1024]{1,0:T(8,128)} %get-tuple-element.283, f32[64,1024]{1,0:T(8,128)S(1)} %gather_fusion, f32[64,1024]{1,0:T(8,128)S(1)} %gather_fusion.1, f32[64]{0:T(128)S(1)} %dynamic-slice_bitcast_fusion.2, s32[64]{0:T(128)S(1)} %get-tuple-element.275, ...), kind=kOutput, calls=%fused_computation.3.clone.1 | convolution fusion | flops 806748160 | bytes 8913472 | tf_op jit(solution)/shard_map/while/body/eval_jaxpr/dot_general | solution.py:56
  70.4 5.4 %copy.95 = f32[1024,1024]{0,1:T(8,128)} copy(f32[1024,1024]{1,0:T(8,128)} %get-tuple-element.283) | data formatting | bytes 8388608 | tf_op jit(solution)/shard_map/while
  78.7 6.8 %convolution_subtract_fusion.2 = f32[1024,1024]{1,0:T(8,128)} fusion(f32[1024,1024]{1,0:T(8,128)} %get-tuple-element.283, f32[64,1024]{1,0:T(8,128)S(1)} %gather_fusion, f32[64,1024]{1,0:T(8,128)S(1)} %gather_fusion.1, f32[64]{0:T(128)S(1)} %dynamic-slice_bitcast_fusion.2, s32[64]{0:T(128)S(1)} %get-tuple-element.275, ...), kind=kOutput, calls=%fused_computation.3.clone.1 | convolution fusion | flops 806748160 | bytes 8913472 | tf_op jit(solution)/shard_map/while/body/eval_jaxpr/dot_general | solution.py:56
  85.5 3.8 %fusion.28 = f32[1024,1024]{0,1:T(8,128)} fusion(f32[64,1024]{1,0:T(8,128)S(1)} %copy-done, s32[1024]{0:T(1024)S(1)} %bitcast.209), kind=kOutput, calls=%fused_computation.39 | convolution fusion | flops 805371904 | bytes 4460544 | tf_op jit(solution)/shard_map/dot_general | solution.py:32
  89.3 3.8 %fusion.30 = f32[1024,1024]{0,1:T(8,128)} fusion(f32[64,1024]{1,0:T(8,128)S(1)} %copy-done.3, s32[1024]{0:T(1024)S(1)} %bitcast.210), kind=kOutput, calls=%fused_computation.41 | convolution fusion | flops 805371904 | bytes 4460544 | tf_op jit(solution)/shard_map/dot_general | solution.py:32
  94.2 4.7 %multiply_reduce_fusion = (f32[1024,16]{0,1:T(8,128)S(1)}, f32[1024,16]{0,1:T(8,128)S(1)}) fusion(f32[1024,64,16]{0,2,1:T(8,128)} %bitcast.204, f32[1024,64]{0,1:T(8,128)S(1)} %broadcast_multiply_fusion, f32[1024,64,16]{0,2,1:T(8,128)} %bitcast.205), kind=kLoop, calls=%fused_computation.30 | loop fusion | flops 4161536 | bytes 8781824 | tf_op jit(solution)/shard_map/reduce_sum | solution.py:33
  101.2 3.6 %fusion.50 = f32[1024,16]{0,1:T(8,128)S(1)} fusion(f32[1024,1024]{1,0:T(8,128)S(1)} %copy-done.2, f32[1024,16]{0,1:T(8,128)S(1)} %get-tuple-element.111), kind=kOutput, calls=%fused_computation.234 | convolution fusion | flops 201326592 | bytes 4325376 | tf_op jit(solution)/shard_map/dot_general | solution.py:98
  107.4 5.6 %fusion.19 = f32[16,64,64]{2,1,0:T(8,128)S(1)} fusion(f32[64,16,1024]{2,1,0:T(8,128)S(1)} %get-tuple-element.173, s32[1024]{0:T(1024)S(1)} %bitcast.211), kind=kOutput, calls=%fused_computation.35 | convolution fusion | flops 805371904 | bytes 4460544 | tf_op jit(solution)/shard_map/dot_general | solution.py:38
  113.4 10.0 %all_to_all.29 = f32[1,16,4096]{2,0,1:T(1,128)S(1)} all-to-all(f32[1,16,4096]{2,0,1:T(1,128)S(1)} %broadcast_in_dim_reshape.5), channel_id=1, replica_groups=mesh['grp'=4,'mem'=8] {'grp'}, dimensions={1} | all-to-all | bytes 524288 | tf_op jit(solution)/shard_map/all_to_all | solution.py:66
  126.1 21.8 %psum.7 = f32[8]{0:T(128)S(1)} all-reduce(f32[8]{0:T(128)S(1)} %compare_select_fusion.3), channel_id=1, replica_groups=mesh['grp'=4,'mem'=8] {'mem'}, use_global_device_ids=true, to_apply=%region_3.4 | all-reduce | flops 8 | bytes 64 | tf_op jit(solution)/shard_map/psum | solution.py:107
  149.3 7.4 %fusion.25 = f32[16,64,64]{2,1,0:T(8,128)S(1)} fusion(f32[64,16,1024]{2,1,0:T(8,128)} %get-tuple-element.174, f32[]{:T(128)} %bitcast.34, s32[1024]{0:T(1024)S(1)} %bitcast.212), kind=kOutput, calls=%fused_computation.37 | convolution fusion | flops 805437440 | bytes 4460548 | tf_op jit(solution)/shard_map/dot_general | solution.py:38
  157.1 8.4 %all_to_all.30 = f32[1,16,4096]{2,0,1:T(1,128)S(1)} all-to-all(f32[1,16,4096]{2,0,1:T(1,128)S(1)} %mul.18371), channel_id=1, replica_groups=mesh['grp'=4,'mem'=8] {'grp'}, dimensions={1} | all-to-all | bytes 524288 | tf_op jit(solution)/shard_map/all_to_all | solution.py:65
  166.4 13.6 %all_to_all.31 = f32[8,4,4,512]{3,1,2,0:T(4,128)S(1)} all-to-all(f32[8,4,4,512]{3,1,2,0:T(4,128)S(1)} %fusion.37), channel_id=1, replica_groups=mesh['grp'=4,'mem'=8] {'mem'}, dimensions={0} | all-to-all | bytes 524288 | tf_op jit(solution)/shard_map/all_to_all | solution.py:69
  180.2 34.4 %convolution_add_fusion = f32[4,512,4096]{2,1,0:T(8,128)} fusion(f32[4,512,4096]{2,1,0:T(8,128)} %param.23, f32[32,4,512]{2,0,1:T(8,128)S(1)} %reshape.1409, f32[32,4,4096]{2,1,0:T(4,128)} %all-gather.2.cloned.1.call-done), kind=kOutput, calls=%fused_computation.23 | convolution fusion | flops 3229614080 | bytes 69468160 | tf_op jit(solution)/shard_map/mqr,mqc->qrc/dot_general | solution.py:72
  (89 shorter events, 25.9 us)
Async XLA Ops:
  6.5 79.0 %copy-start = (f32[64,1024]{1,0:T(8,128)S(1)}, f32[64,1024]{1,0:T(8,128)}, u32[]{:S(2)}) copy-start(f32[64,1024]{1,0:T(8,128)} %param.20) | copy-start | bytes 786436
  6.5 173.6 %all-gather.2.cloned.1.call-start = ((), (), s32[]{:S(2)}) async-start(), calls=%async_computation.3 | async-start | bytes 2359296 | tf_op jit(solution)/shard_map/all_gather | solution.py:75
  7.8 4.9 %copy-start.6 = (s32[1,4,64]{2,1,0:T(4,128)S(1)}, s32[1,4,64]{2,1,0:T(4,128)}, u32[]{:S(2)}) copy-start(s32[1,4,64]{2,1,0:T(4,128)} %param.16) | copy-start | bytes 3076
  7.8 4.9 %copy-start.7 = (s32[1,4,64]{2,1,0:T(4,128)S(1)}, s32[1,4,64]{2,1,0:T(4,128)}, u32[]{:S(2)}) copy-start(s32[1,4,64]{2,1,0:T(4,128)} %param.15) | copy-start | bytes 3076
  7.9 4.9 %copy-start.5 = (s32[1,4,64]{2,1,0:T(4,128)S(1)}, s32[1,4,64]{2,1,0:T(4,128)}, u32[]{:S(2)}) copy-start(s32[1,4,64]{2,1,0:T(4,128)} %param.14) | copy-start | bytes 3076
  12.8 72.7 %copy-start.4 = (s32[1,1024]{1,0:T(1,128)S(1)}, s32[1,1024]{1,0:T(1,128)}, u32[]{:S(2)}) copy-start(s32[1,1024]{1,0:T(1,128)} %param.17) | copy-start | bytes 12292
  85.5 3.8 %copy-start.3 = (f32[64,1024]{1,0:T(8,128)S(1)}, f32[64,1024]{1,0:T(8,128)}, u32[]{:S(2)}) copy-start(f32[64,1024]{1,0:T(8,128)} %param.19) | copy-start | bytes 786436
  94.1 4.7 %copy-start.2 = (f32[1024,1024]{1,0:T(8,128)S(1)}, f32[1024,1024]{1,0:T(8,128)}, u32[]{:S(2)}) copy-start(f32[1024,1024]{1,0:T(8,128)} %get-tuple-element.99) | copy-start | bytes 12582916
  180.2 34.4 %copy-start.1 = (f32[64,1024]{1,0:T(8,128)S(1)}, f32[64,1024]{1,0:T(8,128)}, u32[]{:S(2)}) copy-start(f32[64,1024]{1,0:T(8,128)} %param.20) | copy-start | bytes 786436
Sparse Core Ops, SparseCore 0:
  124.9 51.0 all-gather.1
